TPU v7x, 512 devices: a whole 4x4x16 slice. The times are simulated.
512 devices in a mesh: rep: 4 (over y), blk: 32 (over z, core), tp: 4 (over x).
Axes of the slice: x: 4, y: 4, z: 16, core: 2. Of those that a mesh axis runs over, the one named last changes fastest.
Arguments:
- hidden: bfloat16 [16, 2048], P('rep', 'blk'), may hold values from -64 to 64
- ln_gain: float32 [2, 2048], P(None, 'blk'), may hold values from 0.1 to 1.9
- w_qkv: bfloat16 [2, 2048, 3, 2048], P(None, 'blk', None, 'tp'), may hold values from -0.125 to 0.125
- w_fc1: bfloat16 [2, 2048, 8192], P(None, 'blk', 'tp'), may hold values from -0.125 to 0.125
- w_out: bfloat16 [2, 2048, 2048], P(None, 'tp', 'blk'), may hold values from -0.125 to 0.125
- w_fc2: bfloat16 [2, 8192, 2048], P(None, 'tp', 'blk'), may hold values from -0.0625 to 0.0625
- caches: bfloat16 [2, 2, 1024, 32, 2048], P(None, None, ('rep', 'blk'), None, 'tp'), may hold values from -110 to 110
- page_owner: int32 [1024], P(('rep', 'blk')), may hold values from 0 to 15, as said below
- page_used: int32 [1024], P(('rep', 'blk')), may hold values from 0 to 1, as said below
- page_fill: int32 [1024], P(('rep', 'blk')), may hold values from 0 to 32, as said below
- page_tail: int32 [1024], P(('rep', 'blk')), may hold values from 0 to 1
- positions: int32 [16], P('rep'), may hold values from 0 to 4095
Outputs:
- hidden_out: bfloat16 [16, 2048], P('rep', 'blk')
- caches_out: bfloat16 [2, 2, 1024, 32, 2048], P(None, None, ('rep', 'blk'), None, 'tp')
Inputs may be any that keep to these rules, and one draw needn't show every extreme that they name: `page_owner`: requests are numbered replica by replica, 4 to a replica. Each request has exactly one page with page_tail 1, which is used and lies among the pages of its own replica; other pages of a request may lie on any replica. `page_used`: every page with page_tail 1 is used. `page_fill`: A used page with page_tail 0 is full; a page with page_tail 1 holds fewer than 32 tokens; an unused page holds 0.
All inputs are finite; a program needn't handle non-finite values.
Results may differ from a plain program's by a relative error of at most 0.012.
The roundings to bfloat16 on the way count: a program that leaves them out, or rounds other values in their place, can miss the bound.
Values may be sent and summed in bfloat16 or wider, within the bound.
No kernel may reach another device: no remote copies, remote signals or barrier semaphores. Data moves between devices by JAX's collectives and lax.ppermute only.
A program may use at most 64 MiB of HBM per device.

v0:
```python
import jax
import jax.numpy as jnp
from jax import lax
from jax.sharding import PartitionSpec as P

D = 2048
HD = 64
ROT = 32
LAYERS = 2
PAGE = 32
EPSILON = 1e-05
LOWEST = -1e30


def combined_all(value, axis, join):
    pieces = jax.tree.map(lambda part: lax.all_gather(part, axis), value)
    head = jax.tree.map(lambda part: part[0], pieces)
    tail = jax.tree.map(lambda part: part[1:], pieces)
    so_far, _ = lax.scan(lambda so_far, piece: (join(so_far, piece), None), head, tail)
    return so_far


def rotate_heads(tensor, positions):
    half_rot = ROT // 2
    steps_f = jnp.arange(half_rot, dtype=jnp.float32)
    inverse = 10000.0 ** (-2.0 * steps_f / ROT)
    angles = positions.astype(jnp.float32)[:, None] * inverse[None, :]
    cosine = jnp.cos(angles)[:, None, :]
    sine_val = jnp.sin(angles)[:, None, :]
    first_half = tensor[..., :half_rot]
    second_half = tensor[..., half_rot:ROT]
    return jnp.concatenate(
        [
            first_half * cosine - second_half * sine_val,
            second_half * cosine + first_half * sine_val,
            tensor[..., ROT:],
        ],
        axis=-1,
    )


def page_partials(query_rows, key_pages, value_pages, valid):
    scores = jnp.einsum(
        "shd,sphd->shp", query_rows, key_pages, preferred_element_type=jnp.float32
    ) * HD ** (-0.5)
    scores = jnp.where(valid[:, None, :], scores, LOWEST)
    highest = jnp.max(scores, axis=-1)
    weights = jnp.where(valid[:, None, :], jnp.exp(scores - highest[..., None]), 0.0)
    totals = jnp.sum(weights, axis=-1)
    rounded = weights.astype(jnp.bfloat16)
    outputs = jnp.einsum("shp,sphd->shd", rounded, value_pages, preferred_element_type=jnp.float32)
    return (highest, totals, outputs)


def merge_parts(left_part, right_part):
    left_high, left_total, left_out = left_part
    right_high, right_total, right_out = right_part
    joined = jnp.maximum(left_high, right_high)
    left_factor = jnp.exp(left_high - joined)
    right_factor = jnp.exp(right_high - joined)
    return (
        joined,
        left_total * left_factor + right_total * right_factor,
        left_out * left_factor[..., None] + right_out * right_factor[..., None],
    )


def per_device(
    hidden,
    ln_gain,
    w_qkv,
    w_fc1,
    w_out,
    w_fc2,
    caches,
    page_owner,
    page_used,
    page_fill,
    page_tail,
    positions,
):
    req_rows = hidden.shape[0]
    slot_count = page_owner.shape[0]
    width = w_out.shape[1]
    heads = width // HD
    rep_count = lax.axis_size("rep")
    rep_index = lax.axis_index("rep")
    all_reqs = req_rows * rep_count
    offsets = jnp.arange(PAGE, dtype=jnp.int32)
    is_tail = page_tail == 1
    is_used = page_used == 1
    write_at = (offsets[None, :] == page_fill[:, None]) & is_tail[:, None]
    valid = is_used[:, None] & (offsets[None, :] < (page_fill + page_tail)[:, None])
    home_rows = page_owner - rep_index * req_rows
    pick_home = (
        (home_rows[:, None] == jnp.arange(req_rows, dtype=jnp.int32)[None, :]) & is_tail[:, None]
    ).astype(jnp.bfloat16)
    pick_owner = page_owner[:, None] == jnp.arange(all_reqs, dtype=jnp.int32)[None, :]
    pick_query = pick_owner.astype(jnp.bfloat16)
    own_mask = pick_owner & is_used[:, None]
    own_map = own_mask.astype(jnp.float32)
    state = hidden
    cache_list = []
    for layer in range(LAYERS):
        resid = state.astype(jnp.float32)
        average = lax.psum(jnp.sum(resid, axis=-1), "blk") / D
        centered = resid - average[:, None]
        variance = lax.psum(jnp.sum(centered * centered, axis=-1), "blk") / D
        normed = (
            centered * lax.rsqrt(variance + EPSILON)[:, None] * ln_gain[layer][None, :]
        ).astype(jnp.bfloat16)
        qkv_part = jnp.dot(
            normed,
            w_qkv[layer].reshape(normed.shape[1], 3 * width),
            preferred_element_type=jnp.float32,
        )
        inner_part = jnp.dot(normed, w_fc1[layer], preferred_element_type=jnp.float32)
        qkv_full, inner = lax.psum((qkv_part, inner_part), "blk")
        mlp_act = jax.nn.gelu(inner, approximate=True).astype(jnp.bfloat16)
        qkv_full = qkv_full.reshape(req_rows, 3, heads, HD)
        mlp_part = jnp.dot(mlp_act, w_fc2[layer], preferred_element_type=jnp.float32)
        queries = (
            rotate_heads(qkv_full[:, 0], positions).astype(jnp.bfloat16).reshape(req_rows, width)
        )
        new_keys = (
            rotate_heads(qkv_full[:, 1], positions).astype(jnp.bfloat16).reshape(req_rows, width)
        )
        new_values = qkv_full[:, 2].astype(jnp.bfloat16).reshape(req_rows, width)
        gathered = lax.all_gather(queries, "rep", axis=0, tiled=True)
        fresh = jnp.dot(
            pick_home,
            jnp.concatenate([new_keys, new_values], axis=1),
            preferred_element_type=jnp.float32,
        ).astype(jnp.bfloat16)
        key_pages = jnp.where(write_at[:, :, None], fresh[:, None, :width], caches[layer, 0])
        value_pages = jnp.where(write_at[:, :, None], fresh[:, None, width:], caches[layer, 1])
        cache_list.append(jnp.stack([key_pages, value_pages]))
        query_rows = (
            jnp.dot(pick_query, gathered, preferred_element_type=jnp.float32)
            .astype(jnp.bfloat16)
            .reshape(slot_count, heads, HD)
        )
        highest, totals, outputs = page_partials(
            query_rows,
            key_pages.reshape(slot_count, PAGE, heads, HD),
            value_pages.reshape(slot_count, PAGE, heads, HD),
            valid,
        )
        masked_high = jnp.where(is_used[:, None], highest, LOWEST)
        local_high = jnp.max(
            jnp.where(own_mask[:, :, None], masked_high[:, None, :], LOWEST), axis=0
        )
        slot_high = jnp.sum(jnp.where(own_mask[:, :, None], local_high[None, :, :], 0.0), axis=1)
        scale_w = jnp.where(is_used[:, None], jnp.exp(highest - slot_high), 0.0)
        local_total = jnp.einsum(
            "sr,sh->rh", own_map, totals * scale_w, precision=lax.Precision.HIGHEST
        )
        local_out = jnp.einsum(
            "sr,shd->rhd", own_map, outputs * scale_w[..., None], precision=lax.Precision.HIGHEST
        )
        merged_high, merged_total, merged_out = combined_all(
            (local_high, local_total, local_out), ("rep", "blk"), merge_parts
        )
        req_total = lax.dynamic_slice_in_dim(merged_total, rep_index * req_rows, req_rows, 0)
        req_out = lax.dynamic_slice_in_dim(merged_out, rep_index * req_rows, req_rows, 0)
        attended = (req_out / req_total[..., None]).reshape(req_rows, width).astype(jnp.bfloat16)
        attn_part = jnp.dot(attended, w_out[layer], preferred_element_type=jnp.float32)
        branch_total = lax.psum(attn_part + mlp_part, "tp")
        state = (resid + branch_total).astype(jnp.bfloat16)
    return (state, jnp.stack(cache_list))


def solution(mesh):
    in_specs = (
        P("rep", "blk"),
        P(None, "blk"),
        P(None, "blk", None, "tp"),
        P(None, "blk", "tp"),
        P(None, "tp", "blk"),
        P(None, "tp", "blk"),
        P(None, None, ("rep", "blk"), None, "tp"),
        P(("rep", "blk")),
        P(("rep", "blk")),
        P(("rep", "blk")),
        P(("rep", "blk")),
        P("rep"),
    )
    out_specs = (P("rep", "blk"), P(None, None, ("rep", "blk"), None, "tp"))
    return jax.shard_map(
        per_device, mesh=mesh, in_specs=in_specs, out_specs=out_specs, check_vma=False
    )
```

profile of v0, /device:TPU:2, one launch (start us, length us, event | category | flops | bytes accessed | tf_op | source)
XLA Modules:
  0.0 1091.6 jit_solution(14421208025836142521)
XLA Ops:
  8.0 54.7 %psum.70 = f32[4]{0:T(128)S(1)} all-reduce(f32[4]{0:T(128)S(1)} %convert_reduce_fusion.1), channel_id=1, replica_groups=mesh['rep'=4,'blk'=32,'tp'=4] {'blk'}, use_global_device_ids=true, to_apply=%region_1.0 | all-reduce | flops 4 | bytes 32 | tf_op jit(solution)/shard_map/psum | solution.py:106
  63.6 45.8 %psum.71 = f32[4]{0:T(128)S(1)} all-reduce(f32[4]{0:T(128)S(1)} %fusion.97), channel_id=1, replica_groups=mesh['rep'=4,'blk'=32,'tp'=4] {'blk'}, use_global_device_ids=true, to_apply=%region_3.0 | all-reduce | flops 4 | bytes 32 | tf_op jit(solution)/shard_map/psum | solution.py:108
  111.5 1.2 fusion.20
  113.6 90.1 %all-reduce.1 = (f32[4,3,8,64]{3,2,1,0:T(8,128)S(1)}, f32[4,2048]{1,0:T(4,128)S(1)}) all-reduce(f32[4,3,8,64]{3,2,1,0:T(8,128)S(1)} %reshape.328, f32[4,2048]{1,0:T(4,128)S(1)} %fusion.20), channel_id=1, replica_groups=mesh['rep'=4,'blk'=32,'tp'=4] {'blk'}, use_global_device_ids=true, to_apply=%region_4.0 | all-reduce | flops 14336 | bytes 114688 | tf_op jit(solution)/shard_map/psum | solution.py:118
  209.5 12.4 %all-gather.6 = bf16[4,4,512]{2,1,0:T(4,128)(2,1)S(1)} all-gather(bf16[1,4,512]{2,1,0:T(4,128)(2,1)S(1)} %reshape.356), channel_id=1, replica_groups=mesh['rep'=4,'blk'=32,'tp'=4] {'rep'}, dimensions={0}, use_global_device_ids=true | all-gather | bytes 20480 | tf_op jit(solution)/shard_map/all_gather | solution.py:129
  223.1 1.3 fusion.131
  229.0 82.1 %all-gather.8 = f32[128,16,8]{1,2,0:T(8,128)S(1)} all-gather(f32[1,16,8]{1,2,0:T(8,128)S(1)} %convolution_bitcast_fusion.1), channel_id=3, replica_groups=mesh['rep'=4,'blk'=32,'tp'=4] {'rep','blk'}, dimensions={0}, use_global_device_ids=true | all-gather | bytes 66048 | tf_op jit(solution)/shard_map/all_gather | solution.py:16
  311.2 80.5 %all-gather.7 = f32[128,16,8]{1,2,0:T(8,128)S(1)} all-gather(f32[1,16,8]{1,2,0:T(8,128)S(1)} %bitcast.159), channel_id=2, replica_groups=mesh['rep'=4,'blk'=32,'tp'=4] {'rep','blk'}, dimensions={0}, use_global_device_ids=true | all-gather | bytes 66048 | tf_op jit(solution)/shard_map/all_gather | solution.py:16
  392.7 7.1 slice.234
  399.8 145.0 %while.28 = (s32[]{:T(128)}, f32[16,8]{0,1:T(8,128)S(1)}, f32[16,8]{0,1:T(8,128)S(1)}, f32[16,8,64]{2,1,0:T(8,128)S(1)}, f32[127,16,8]{1,2,0:T(8,128)S(1)}, /*in...) while((s32[]{:T(128)}, f32[16,8]{0,1:T(8,128)S(1)}, f32[16,8]{0,1:T(8,128)S(1)}, ...), condition=%wide.region_10.11_spmd, body=%wide.region_9.10_spmd.sunk | while | flops 25346 | bytes 171109 | solution.py:19
  545.3 1.1 convolution_add_fusion.1
  546.4 8.6 psum.74
  555.1 46.2 %psum.75 = f32[4]{0:T(128)S(1)} all-reduce(f32[4]{0:T(128)S(1)} %get-tuple-element.178), channel_id=1, replica_groups=mesh['rep'=4,'blk'=32,'tp'=4] {'blk'}, use_global_device_ids=true, to_apply=%region_14.15 | all-reduce | flops 4 | bytes 32 | tf_op jit(solution)/shard_map/psum | solution.py:106
  601.8 45.8 %psum.76 = f32[4]{0:T(128)S(1)} all-reduce(f32[4]{0:T(128)S(1)} %fusion.94), channel_id=1, replica_groups=mesh['rep'=4,'blk'=32,'tp'=4] {'blk'}, use_global_device_ids=true, to_apply=%region_16.17 | all-reduce | flops 4 | bytes 32 | tf_op jit(solution)/shard_map/psum | solution.py:108
  647.6 1.2 fusion.17
  648.7 1.1 fusion.122
  650.0 90.3 %all-reduce = (f32[4,3,8,64]{3,2,0,1:T(8,128)S(1)}, f32[4,2048]{1,0:T(4,128)S(1)}) all-reduce(f32[4,3,8,64]{3,2,0,1:T(8,128)S(1)} %copy.83, f32[4,2048]{1,0:T(4,128)S(1)} %fusion.17), channel_id=1, replica_groups=mesh['rep'=4,'blk'=32,'tp'=4] {'blk'}, use_global_device_ids=true, to_apply=%region_17.18 | all-reduce | flops 14336 | bytes 114688 | tf_op jit(solution)/shard_map/psum | solution.py:118
  741.2 11.9 %all-gather.9 = bf16[4,4,512]{2,1,0:T(4,128)(2,1)S(1)} all-gather(bf16[1,4,512]{2,1,0:T(4,128)(2,1)S(1)} %reshape.362), channel_id=1, replica_groups=mesh['rep'=4,'blk'=32,'tp'=4] {'rep'}, dimensions={0}, use_global_device_ids=true | all-gather | bytes 20480 | tf_op jit(solution)/shard_map/all_gather | solution.py:129
  756.4 81.7 %all-gather.11 = f32[128,16,8]{1,2,0:T(8,128)S(1)} all-gather(f32[1,16,8]{1,2,0:T(8,128)S(1)} %convolution_bitcast_fusion), channel_id=6, replica_groups=mesh['rep'=4,'blk'=32,'tp'=4] {'rep','blk'}, dimensions={0}, use_global_device_ids=true | all-gather | bytes 66048 | tf_op jit(solution)/shard_map/all_gather | solution.py:16
  838.2 80.9 %all-gather.10 = f32[128,16,8]{1,2,0:T(8,128)S(1)} all-gather(f32[1,16,8]{1,2,0:T(8,128)S(1)} %bitcast.160), channel_id=5, replica_groups=mesh['rep'=4,'blk'=32,'tp'=4] {'rep','blk'}, dimensions={0}, use_global_device_ids=true | all-gather | bytes 66048 | tf_op jit(solution)/shard_map/all_gather | solution.py:16
  919.4 1.1 pad_maximum_fusion
  921.4 7.2 slice.251
  928.5 144.9 %while.29 = (s32[]{:T(128)}, f32[16,8]{0,1:T(8,128)S(1)}, f32[16,8]{0,1:T(8,128)S(1)}, f32[16,8,64]{2,1,0:T(8,128)S(1)}, f32[127,16,8]{1,2,0:T(8,128)S(1)}, /*in...) while((s32[]{:T(128)}, f32[16,8]{0,1:T(8,128)S(1)}, f32[16,8]{0,1:T(8,128)S(1)}, ...), condition=%wide.region_23.24_spmd, body=%wide.region_22.23_spmd.sunk | while | flops 25346 | bytes 171109 | solution.py:19
  1074.1 10.1 psum.79
  (1404 shorter events, 308.3 us)
Async XLA Ops:
  7.2 219.5 %copy-start.4 = (s32[8]{0:T(128)S(1)}, s32[8]{0:T(128)}, u32[]{:S(2)}) copy-start(s32[8]{0:T(128)} %param.23) | copy-start | bytes 100
  7.2 384.6 %all-gather.15.cloned.1.call-start = ((), (), s32[]{:S(2)}) async-start(), calls=%async_computation | async-start | bytes 8454144 | tf_op jit(solution)/shard_map/all_gather | solution.py:16
  227.6 692.9 %all-gather.17.cloned.1.call-start = ((), (), s32[]{:S(2)}) async-start(), calls=%async_computation.1 | async-start | bytes 8454144 | tf_op jit(solution)/shard_map/all_gather | solution.py:16
  392.6 152.5 %copy-start.1 = (bf16[2,512,64]{1,2,0:T(8,128)(2,1)S(1)}, bf16[2,512,64]{1,2,0:T(8,128)(2,1)}, u32[]{:S(2)}) copy-start(bf16[2,512,64]{1,2,0:T(8,128)(2,1)} %param.20) | copy-start | bytes 393220
  392.6 162.3 %copy-start.3 = (bf16[4,64]{1,0:T(4,128)(2,1)S(1)}, bf16[4,64]{1,0:T(4,128)(2,1)}, u32[]{:S(2)}) copy-start(bf16[4,64]{1,0:T(4,128)(2,1)} %param.16) | copy-start | bytes 1540
  399.8 519.3 %copy-start = (bf16[2,2,8,32,512]{4,3,2,1,0:T(8,128)(2,1)S(1)}, bf16[2,2,8,32,512]{4,3,2,1,0:T(8,128)(2,1)}, u32[]{:S(2)}) copy-start(bf16[2,2,8,32,512]{4,3,2,1,0:T(8,128)(2,1)} %param.22) | copy-start | bytes 3145732
  921.3 152.4 %copy-start.2 = (bf16[2,512,64]{1,2,0:T(8,128)(2,1)S(1)}, bf16[2,512,64]{1,2,0:T(8,128)(2,1)}, u32[]{:S(2)}) copy-start(bf16[2,512,64]{1,2,0:T(8,128)(2,1)} %param.20) | copy-start | bytes 393220
  921.3 152.5 %copy-start.5 = (bf16[2,2048,64]{1,2,0:T(8,128)(2,1)S(1)}, bf16[2,2048,64]{1,2,0:T(8,128)(2,1)}, u32[]{:S(2)}) copy-start(bf16[2,2048,64]{1,2,0:T(8,128)(2,1)} %param.21) | copy-start | bytes 1572868
Sparse Core Ops, SparseCore 0:
  227.7 143.5 all-gather.14
  756.4 142.3 all-gather.16
where the time goes:
time: 1100 us; the launch traced here: 1090 us
  blocking collectives  741 us (67%)
  local copies, waits for them, and re-layouts  275 us (25%)
  other arithmetic  43.7 us (4%)
  between operations  14.3 us (1%)
    all_gather x4, blocking collectives, combined_all(): pieces = jax.tree.map(lambda part: lax.all_gather(part, axis), value)  325 us
    dynamic_slice x254, local copies, waits for them, and re-layouts, combined_all(): lax.scan(lambda so_far, piece: (join(so_far, piece), None), head, tail)  215 us
    psum x2, blocking collectives, per_device(): qkv_full, inner = lax.psum((qkv_part, inner_part), 'blk')  180 us
    psum x2, blocking collectives, per_device(): average = lax.psum(jnp.sum(resid, axis=-1), 'blk') / D  101 us
    psum x2, blocking collectives, per_device(): variance = lax.psum(jnp.sum(centered * centered, axis=-1), 'blk') / D  91.6 us
    add x254, other arithmetic, merge_parts(): left_out * left_factor[..., None] + right_out * right_factor[..., None]  28.1 us
    all_gather x2, blocking collectives, per_device(): gathered = lax.all_gather(queries, 'rep', axis=0, tiled=True)  24.4 us
  transfers between devices with their start and end apart: 2, of which 0 were waited for; matrix products, arithmetic and copies ran while one was open for 0% of the time, Pallas kernels for 0%

commit v1 on v0

--- a/solution.py
+++ b/solution.py
@@ -10,6 +10,27 @@
 PAGE = 32
 EPSILON = 1e-05
 LOWEST = -1e30
+
+
+def ring_gather(x, axis, dim):
+    peers, index, width = (lax.axis_size(axis), lax.axis_index(axis), x.shape[dim])
+    right = [(i, (i + 1) % peers) for i in range(peers)]
+    behind = [(i, (i - 1) % peers) for i in range(peers)]
+    filled = jnp.zeros((*x.shape[:dim], peers * width, *x.shape[dim + 1 :]), x.dtype)
+    filled = lax.dynamic_update_slice_in_dim(filled, x, index * width, axis=dim)
+    from_left = from_right = x
+    halfway = peers // 2
+    for turn in range(1, halfway + 1):
+        from_left = lax.ppermute(from_left, axis, right)
+        filled = lax.dynamic_update_slice_in_dim(
+            filled, from_left, (index - turn) % peers * width, axis=dim
+        )
+        if turn < peers - halfway:
+            from_right = lax.ppermute(from_right, axis, behind)
+            filled = lax.dynamic_update_slice_in_dim(
+                filled, from_right, (index + turn) % peers * width, axis=dim
+            )
+    return filled
 
 
 def combined_all(value, axis, join):
@@ -126,7 +147,7 @@
             rotate_heads(qkv_full[:, 1], positions).astype(jnp.bfloat16).reshape(req_rows, width)
         )
         new_values = qkv_full[:, 2].astype(jnp.bfloat16).reshape(req_rows, width)
-        gathered = lax.all_gather(queries, "rep", axis=0, tiled=True)
+        gathered = ring_gather(queries, "rep", 0)
         fresh = jnp.dot(
             pick_home,
             jnp.concatenate([new_keys, new_values], axis=1),

time: 1100 us -> 1110 us (level)
  blocking collectives: 741 us -> 716 us
  starting transfers between devices: 0.08 us -> 17.1 us
  waiting for transfers between devices: 0.05 us -> 12.6 us
    all_gather x2 -> x0, blocking collectives: 24.4 us -> none  [per_device(): gathered = lax.all_gather(queries, 'rep', axis=0, tiled=True)]
    ppermute x0 -> x6, starting transfers between devices: none -> 17.1 us  [the longest x2 8.78 us: ring_gather(): from_right = lax.ppermute(from_right, axis, behind)]
    ppermute x0 -> x6, waiting for transfers between devices: none -> 12.5 us  [the longest x4 12.5 us: ring_gather(): from_left = lax.ppermute(from_left, axis, right)]
  transfers between devices with their start and end apart: 2 -> 8, of which waited for: 0 -> 3; matrix products, arithmetic and copies ran while one was open for 0% -> 1% of each run, Pallas kernels for 0% -> 0%
where the time goes in v1:
time: 1110 us; the launch traced here: 1100 us
  blocking collectives  716 us (65%)
  local copies, waits for them, and re-layouts  275 us (25%)
  other arithmetic  44 us (4%)
  starting transfers between devices  17.1 us (2%)
  between operations  14.5 us (1%)
  waiting for transfers between devices  12.6 us (1%)
    all_gather x4, blocking collectives, combined_all(): pieces = jax.tree.map(lambda part: lax.all_gather(part, axis), value)  325 us
    dynamic_slice x254, local copies, waits for them, and re-layouts, combined_all(): lax.scan(lambda so_far, piece: (join(so_far, piece), None), head, tail)  215 us
    psum x2, blocking collectives, per_device(): qkv_full, inner = lax.psum((qkv_part, inner_part), 'blk')  180 us
    psum x2, blocking collectives, per_device(): average = lax.psum(jnp.sum(resid, axis=-1), 'blk') / D  101 us
    psum x2, blocking collectives, per_device(): variance = lax.psum(jnp.sum(centered * centered, axis=-1), 'blk') / D  91.6 us
    add x254, other arithmetic, merge_parts(): left_out * left_factor[..., None] + right_out * right_factor[..., None]  28.1 us
  transfers between devices with their start and end apart: 8, of which 3 were waited for; matrix products, arithmetic and copies ran while one was open for 1% of the time, Pallas kernels for 0%

profile of v1, /device:TPU:2, one launch (start us, length us, event | category | flops | bytes accessed | tf_op | source)
XLA Modules:
  0.0 1096.5 jit_solution(12080901201417976945)
XLA Ops:
  8.0 54.7 %psum.70 = f32[4]{0:T(128)S(1)} all-reduce(f32[4]{0:T(128)S(1)} %convert_reduce_fusion.1), channel_id=1, replica_groups=mesh['rep'=4,'blk'=32,'tp'=4] {'blk'}, use_global_device_ids=true, to_apply=%region_1.0 | all-reduce | flops 4 | bytes 32 | tf_op jit(solution)/shard_map/psum | solution.py:127
  64.3 45.8 %psum.71 = f32[4]{0:T(128)S(1)} all-reduce(f32[4]{0:T(128)S(1)} %fusion.97), channel_id=1, replica_groups=mesh['rep'=4,'blk'=32,'tp'=4] {'blk'}, use_global_device_ids=true, to_apply=%region_3.0 | all-reduce | flops 4 | bytes 32 | tf_op jit(solution)/shard_map/psum | solution.py:129
  114.3 90.1 %all-reduce.1 = (f32[4,3,8,64]{3,2,1,0:T(8,128)S(1)}, f32[4,2048]{1,0:T(4,128)}) all-reduce(f32[4,3,8,64]{3,2,1,0:T(8,128)S(1)} %reshape.328, f32[4,2048]{1,0:T(4,128)S(1)} %fusion.20), channel_id=1, replica_groups=mesh['rep'=4,'blk'=32,'tp'=4] {'blk'}, use_global_device_ids=true, to_apply=%region_4.0 | all-reduce | flops 14336 | bytes 114688 | tf_op jit(solution)/shard_map/psum | solution.py:139
  204.9 4.9 collective-permute-start.1
  209.8 1.9 collective-permute-start
  218.9 2.5 collective-permute-start.2
  221.5 4.2 collective-permute-done.2
  229.6 81.7 %all-gather.7 = f32[128,16,8]{1,2,0:T(8,128)S(1)} all-gather(f32[1,16,8]{1,2,0:T(8,128)S(1)} %convolution_bitcast_fusion.1), channel_id=3, replica_groups=mesh['rep'=4,'blk'=32,'tp'=4] {'rep','blk'}, dimensions={0}, use_global_device_ids=true | all-gather | bytes 66048 | tf_op jit(solution)/shard_map/all_gather | solution.py:37
  311.3 81.0 %all-gather.6 = f32[128,16,8]{1,2,0:T(8,128)S(1)} all-gather(f32[1,16,8]{1,2,0:T(8,128)S(1)} %bitcast.160), channel_id=2, replica_groups=mesh['rep'=4,'blk'=32,'tp'=4] {'rep','blk'}, dimensions={0}, use_global_device_ids=true | all-gather | bytes 66048 | tf_op jit(solution)/shard_map/all_gather | solution.py:37
  393.3 7.2 slice.234
  400.4 145.3 %while.28 = (s32[]{:T(128)}, f32[16,8]{0,1:T(8,128)S(1)}, f32[16,8]{0,1:T(8,128)S(1)}, f32[16,8,64]{2,1,0:T(8,128)S(1)}, f32[127,16,8]{1,2,0:T(8,128)S(1)}, /*in...) while((s32[]{:T(128)}, f32[16,8]{0,1:T(8,128)S(1)}, f32[16,8]{0,1:T(8,128)S(1)}, ...), condition=%wide.region_10.11_spmd, body=%wide.region_9.10_spmd.sunk | while | flops 25346 | bytes 171109 | solution.py:40
  547.3 8.6 psum.74
  556.0 45.8 %psum.75 = f32[4]{0:T(128)S(1)} all-reduce(f32[4]{0:T(128)S(1)} %get-tuple-element.178), channel_id=1, replica_groups=mesh['rep'=4,'blk'=32,'tp'=4] {'blk'}, use_global_device_ids=true, to_apply=%region_14.15 | all-reduce | flops 4 | bytes 32 | tf_op jit(solution)/shard_map/psum | solution.py:127
  602.3 45.8 %psum.76 = f32[4]{0:T(128)S(1)} all-reduce(f32[4]{0:T(128)S(1)} %fusion.94), channel_id=1, replica_groups=mesh['rep'=4,'blk'=32,'tp'=4] {'blk'}, use_global_device_ids=true, to_apply=%region_16.17 | all-reduce | flops 4 | bytes 32 | tf_op jit(solution)/shard_map/psum | solution.py:129
  650.5 90.3 %all-reduce = (f32[4,3,8,64]{3,2,0,1:T(8,128)S(1)}, f32[4,2048]{1,0:T(4,128)S(1)}) all-reduce(f32[4,3,8,64]{3,2,0,1:T(8,128)S(1)} %copy.83, f32[4,2048]{1,0:T(4,128)S(1)} %fusion.17), channel_id=1, replica_groups=mesh['rep'=4,'blk'=32,'tp'=4] {'blk'}, use_global_device_ids=true, to_apply=%region_17.18 | all-reduce | flops 14336 | bytes 114688 | tf_op jit(solution)/shard_map/psum | solution.py:139
  741.2 3.9 collective-permute-start.4
  745.1 2.0 collective-permute-start.3
  748.2 3.6 collective-permute-done.3
  753.8 4.7 collective-permute-done.5
  762.6 79.6 %all-gather.9 = f32[128,16,8]{1,2,0:T(8,128)S(1)} all-gather(f32[1,16,8]{1,2,0:T(8,128)S(1)} %convolution_bitcast_fusion), channel_id=6, replica_groups=mesh['rep'=4,'blk'=32,'tp'=4] {'rep','blk'}, dimensions={0}, use_global_device_ids=true | all-gather | bytes 66048 | tf_op jit(solution)/shard_map/all_gather | solution.py:37
  842.3 82.9 %all-gather.8 = f32[128,16,8]{1,2,0:T(8,128)S(1)} all-gather(f32[1,16,8]{1,2,0:T(8,128)S(1)} %bitcast.159), channel_id=5, replica_groups=mesh['rep'=4,'blk'=32,'tp'=4] {'rep','blk'}, dimensions={0}, use_global_device_ids=true | all-gather | bytes 66048 | tf_op jit(solution)/shard_map/all_gather | solution.py:37
  926.2 7.2 slice.251
  933.4 144.9 %while.29 = (s32[]{:T(128)}, f32[16,8]{0,1:T(8,128)S(1)}, f32[16,8]{0,1:T(8,128)S(1)}, f32[16,8,64]{2,1,0:T(8,128)S(1)}, f32[127,16,8]{1,2,0:T(8,128)S(1)}, /*in...) while((s32[]{:T(128)}, f32[16,8]{0,1:T(8,128)S(1)}, f32[16,8]{0,1:T(8,128)S(1)}, ...), condition=%wide.region_23.24_spmd, body=%wide.region_22.23_spmd.sunk | while | flops 25346 | bytes 171109 | solution.py:40
  1078.9 10.2 psum.79
  (1424 shorter events, 317.0 us)
Async XLA Ops:
  7.2 218.5 %copy-start.4 = (s32[8]{0:T(128)S(1)}, s32[8]{0:T(128)}, u32[]{:S(2)}) copy-start(s32[8]{0:T(128)} %param.23) | copy-start | bytes 100
  7.2 385.2 %all-gather.13.cloned.1.call-start = ((), (), s32[]{:S(2)}) async-start(), calls=%async_computation | async-start | bytes 8454144 | tf_op jit(solution)/shard_map/all_gather | solution.py:37
  204.9 16.5 %collective-permute-start.1 = (bf16[4,512]{1,0:T(4,128)(2,1)S(1)}, bf16[4,512]{1,0:T(4,128)(2,1)S(1)}, u32[]{:S(2)}, u32[]{:S(2)}) collective-permute-start(bf16[4,512]{1,0:T(4,128)(2,1)S(1)} %convert_element_type.96), channel_id=1, source_target_pairs={{0,384},{128,0},{256,128},{384,256},{1,385},{129,1},{257,129},{385... | collective-permute-start | bytes 12296 | tf_op jit(solution)/shard_map/ppermute | solution.py:29
  209.8 9.1 collective-permute-start
  218.9 6.7 collective-permute-start.2
  228.2 697.1 %all-gather.15.cloned.1.call-start = ((), (), s32[]{:S(2)}) async-start(), calls=%async_computation.1 | async-start | bytes 8454144 | tf_op jit(solution)/shard_map/all_gather | solution.py:37
  393.2 152.8 %copy-start.1 = (bf16[2,512,64]{1,2,0:T(8,128)(2,1)S(1)}, bf16[2,512,64]{1,2,0:T(8,128)(2,1)}, u32[]{:S(2)}) copy-start(bf16[2,512,64]{1,2,0:T(8,128)(2,1)} %param.20) | copy-start | bytes 393220
  393.2 153.0 %copy-start.6 = (f32[4,2048]{1,0:T(4,128)S(1)}, f32[4,2048]{1,0:T(4,128)}, u32[]{:S(2)}) copy-start(f32[4,2048]{1,0:T(4,128)} %get-tuple-element.169) | copy-start | bytes 98308
  393.2 162.7 %copy-start.3 = (bf16[4,64]{1,0:T(4,128)(2,1)S(1)}, bf16[4,64]{1,0:T(4,128)(2,1)}, u32[]{:S(2)}) copy-start(bf16[4,64]{1,0:T(4,128)(2,1)} %param.16) | copy-start | bytes 1540
  400.4 360.6 %copy-start = (bf16[2,2,8,32,512]{4,3,2,1,0:T(8,128)(2,1)S(1)}, bf16[2,2,8,32,512]{4,3,2,1,0:T(8,128)(2,1)}, u32[]{:S(2)}) copy-start(bf16[2,2,8,32,512]{4,3,2,1,0:T(8,128)(2,1)} %param.22) | copy-start | bytes 3145732
  741.2 12.5 %collective-permute-start.4 = (bf16[4,512]{1,0:T(4,128)(2,1)S(1)}, bf16[4,512]{1,0:T(4,128)(2,1)S(1)}, u32[]{:S(2)}, u32[]{:S(2)}) collective-permute-start(bf16[4,512]{1,0:T(4,128)(2,1)S(1)} %convert_element_type.108), channel_id=1, source_target_pairs={{0,384},{128,0},{256,128},{384,256},{1,385},{129,1},{257,129},{385... | collective-permute-start | bytes 12296 | tf_op jit(solution)/shard_map/ppermute | solution.py:29
  745.1 6.7 collective-permute-start.3
  751.8 6.7 collective-permute-start.5
  926.2 152.4 %copy-start.2 = (bf16[2,512,64]{1,2,0:T(8,128)(2,1)S(1)}, bf16[2,512,64]{1,2,0:T(8,128)(2,1)}, u32[]{:S(2)}) copy-start(bf16[2,512,64]{1,2,0:T(8,128)(2,1)} %param.20) | copy-start | bytes 393220
  926.2 152.5 %copy-start.5 = (bf16[2,2048,64]{1,2,0:T(8,128)(2,1)S(1)}, bf16[2,2048,64]{1,2,0:T(8,128)(2,1)}, u32[]{:S(2)}) copy-start(bf16[2,2048,64]{1,2,0:T(8,128)(2,1)} %param.21) | copy-start | bytes 1572868
Sparse Core Ops, SparseCore 0:
  228.3 143.2 all-gather.12
  761.2 141.9 all-gather.14
